TPU v7x, 32 devices: a whole 2x2x4 slice. The times are simulated.
32 devices in a mesh: station: 4 (over z), group: 4 (over x, core), bias: 2 (over y).
Axes of the slice: x: 2, y: 2, z: 4, core: 2. Of those that a mesh axis runs over, the one named last changes fastest.
Arguments:
- normal_mat: float32 [128, 2304], P(('station', 'group')), may hold values from -16 to 18, as said below
- coupling: float32 [128, 2, 8, 48, 128], P(('station', 'group'), 'bias'), may hold values from -0.13258252 to 0.13258252
- lengths: int32 [128], P(('station', 'group')), may hold values from 12 to 48
- visible: int32 [128, 2, 8], P(('station', 'group'), 'bias'), may hold values from 0 to 16, as said below
- bias_prior: float32 [2, 16, 128], P('bias', 'station'), may hold values from 0.1 to 1
- unimod: int32 [128, 2304], P(('station', 'group')), may hold values from -1 to 2, as said below
Outputs:
- bias_cov: float32 [2, 16, 128, 128], P('bias', 'station')
- amb_cov: float32 [128, 2304], P(('station', 'group'))
Inputs may be any that keep to these rules, and one draw needn't show every extreme that they name: `normal_mat`: each station's matrix, read as 48 x 48 row by row, is symmetric with all eigenvalues 1 or more. Each list visible[s, h] holds distinct block numbers below 16 in its first slots and the value 16 in its unused slots; every list has at least one block; in every draw the stations of some devices use all 8 slots. `unimod`: each station's matrix, read as 48 x 48 row by row, is a unit lower triangular times a unit upper triangular integer matrix; each row of the lower factor and each column of the upper factor holds at most one entry off the diagonal, -1 or 1; so every leading square block has determinant 1.
All inputs are finite; a program needn't handle non-finite values.
Results may differ from a plain program's by a relative error of at most 0.0003.
Values sent between devices are 32-bit elements; how exact they have to be, the bound alone decides.
No kernel may reach another device: no remote copies, remote signals or barrier semaphores. Data moves between devices by JAX's collectives and lax.ppermute only.
A program may use at most 64 MiB of HBM per device.

v0:
```python
import jax
import jax.numpy as jnp
from jax import lax
from jax.sharding import PartitionSpec as P

NHALF = 16
precise = lax.Precision.HIGHEST


def spd_inverse(matrix):
    matrix_order = matrix.shape[-1]
    factor = jnp.linalg.cholesky(matrix)
    identity = jnp.broadcast_to(jnp.eye(matrix_order, dtype=matrix.dtype), matrix.shape)
    lower_inv = lax.linalg.triangular_solve(factor, identity, left_side=True, lower=True)
    return jnp.einsum("...ka,...kb->...ab", lower_inv, lower_inv, precision=precise)


def prepare(normal_mat, coupling, lengths):
    stations = coupling.shape[0]
    block_len = coupling.shape[3]
    positions = jnp.arange(block_len, dtype=jnp.int32)
    row_valid = (positions[None, :] < lengths[:, None]).astype(jnp.float32)
    keep_mask = row_valid[:, :, None] * row_valid[:, None, :]
    stacked = normal_mat.reshape(stations, block_len, block_len)
    effective = keep_mask * stacked + (1.0 - keep_mask) * jnp.eye(block_len, dtype=jnp.float32)
    inverse = spd_inverse(effective)
    weighted = coupling * row_valid[:, None, None, :, None]
    solved = jnp.einsum("sab,shjbc->shjac", inverse, weighted, precision=precise)
    return (keep_mask, inverse, weighted, solved)


def finish_cov(keep_mask, inverse, bias_part, unimod):
    stations = keep_mask.shape[0]
    block_len = keep_mask.shape[1]
    covariance = keep_mask * (inverse + bias_part)
    integer_map = unimod.reshape(stations, block_len, block_len).astype(jnp.float32)
    mapped = jnp.einsum("sab,sbc,sdc->sad", integer_map, covariance, integer_map, precision=precise)
    return (keep_mask * mapped).reshape(stations, block_len * block_len)


def local(normal_mat, coupling, lengths, visible, bias_prior, unimod):
    keep_mask, inverse, weighted, solved = prepare(normal_mat, coupling, lengths)
    reduced = jnp.einsum("shjac,shjad->shjcd", weighted, weighted - solved, precision=precise)
    block_width = coupling.shape[4]
    identity = jnp.eye(block_width, dtype=jnp.float32)
    columns = jnp.arange(NHALF, dtype=jnp.int32)
    selector = (visible[..., None] == columns).astype(jnp.float32)
    block_table = jnp.einsum("shjx,shjcd->hxcd", selector, reduced, precision=precise)
    local_sum = lax.psum_scatter(block_table, "station", scatter_dimension=1, tiled=True)
    block_sum = lax.psum(local_sum, "group")
    bias_cov = spd_inverse(block_sum + bias_prior[..., :, None] * identity)
    segment = lax.all_gather(bias_cov, "station", axis=1, tiled=True)
    piece_len = segment.shape[1]
    local_pick = (visible[..., None] == jnp.arange(piece_len, dtype=jnp.int32)).astype(jnp.float32)
    chosen = jnp.einsum("shjx,hxcd->shjcd", local_pick, segment, precision=precise)
    lifted = jnp.einsum("shjac,shjcd->shjad", solved, chosen, precision=precise)
    bias_part = jnp.einsum("shjad,shjbd->sab", lifted, solved, precision=precise)
    combined = lax.psum(bias_part.reshape(bias_part.shape[0], -1), "bias")
    amb_cov = finish_cov(keep_mask, inverse, combined.reshape(bias_part.shape), unimod)
    return (bias_cov, amb_cov)


def solution(mesh):
    return jax.shard_map(
        local,
        mesh=mesh,
        in_specs=(
            P(("station", "group"), None),
            P(("station", "group"), "bias", None, None, None),
            P(("station", "group")),
            P(("station", "group"), "bias", None),
            P("bias", "station", None),
            P(("station", "group"), None),
        ),
        out_specs=(P("bias", "station", None, None), P(("station", "group"), None)),
        check_vma=False,
    )
```

profile of v0, /device:TPU:0, one launch (start us, length us, event | category | flops | bytes accessed | tf_op | source)
XLA Modules:
  0.0 314.8 jit_solution(5613608994066356341)
XLA Ops:
  7.2 0.0 reduce-scatter.2.cloned.1.call-start
  7.3 0.7 fusion.43
  8.0 0.1 copy.56
  8.1 1.0 reshape.177
  9.1 0.1 copy.55
  9.2 0.1 fusion.24
  9.3 0.1 copy.57
  9.4 0.1 fusion.30
  9.6 35.2 %custom-call.14 = f32[8,48,48]{2,1,0:T(8,128)S(1)} custom-call(f32[8,48,48]{2,1,0:T(8,128)S(1)} %fusion.30), custom_call_target="Cholesky" | custom-call | tf_op jit(solution)/shard_map/jit(cholesky)/cholesky | solution.py:12
  44.8 0.1 compare_reduce_fusion
  44.9 0.1 select_bitcast_fusion.1
  45.0 29.5 %custom-call.15 = f32[8,1,48,48]{2,3,1,0:T(8,128)S(1)} custom-call(f32[8,1,48,48]{3,2,1,0:T(8,128)S(1)} %select_bitcast_fusion.1), custom_call_target="InvertDiagBlocksLowerTriangular" | custom-call | tf_op jit(solution)/shard_map/triangular_solve | solution.py:14
  74.6 0.5 fusion.28
  75.1 0.5 fusion.44
  75.6 1.7 fusion.10
  77.3 6.9 %fusion.7 = f32[8,8,128,128]{3,2,1,0:T(8,128)S(1)} fusion(f32[8,8,128,48]{2,3,1,0:T(8,128)S(1)} %fusion.10, f32[8,1,8,48,128]{4,3,2,1,0:T(8,128)S(1)} %copy-done, f32[8,48]{1,0:T(8,128)S(1)} %fusion.43), kind=kOutput, calls=%fused_computation.9 | convolution fusion | flops 605159424 | bytes 7341568 | tf_op jit(solution)/shard_map/shjac,shjad->shjcd/dot_general | solution.py:43
  84.2 4.1 %fusion.12 = f32[16,128,128]{2,0,1:T(8,128)S(1)} fusion(f32[8,8,128,128]{3,2,1,0:T(8,128)S(1)} %fusion.7, s32[8,8]{1,0:T(8,128)S(1)} %bitcast.86), kind=kOutput, calls=%fused_computation.14 | convolution fusion | flops 201327616 | bytes 5243136 | tf_op jit(solution)/shard_map/shjx,shjcd->hxcd/dot_general | solution.py:48
  88.3 1.4 copy.62
  89.8 0.0 reduce-scatter.2.cloned.1.call-update
  89.8 0.0 all-reduce.3.cloned.1.call-start
  89.9 30.1 %reduce-scatter.2.cloned.1.call-done = f32[1,4,128,128]{2,3,1,0:T(8,128)} async-done(((f32[1,16,128,128]{2,3,1,0:T(8,128)}), f32[1,4,128,128]{2,3,1,0:T(8,128)}) %reduce-scatter.2.cloned.1.call-update) | async-done | bytes 262160 | tf_op jit(solution)/shard_map/reduce_scatter | solution.py:49
  120.0 0.0 all-reduce.3.cloned.1.call-update
  120.0 0.0 all-gather.3.cloned.1.call-start
  120.1 0.1 copy.63
  120.2 32.9 %all-reduce.3.cloned.1.call-done = f32[1,4,128,128]{2,3,1,0:T(8,128)} async-done(((f32[1,4,128,128]{2,3,1,0:T(8,128)}), f32[1,4,128,128]{2,3,1,0:T(8,128)}) %all-reduce.3.cloned.1.call-update) | async-done | bytes 262160 | tf_op jit(solution)/shard_map/psum | solution.py:50
  153.1 1.0 multiply_add_fusion
  154.1 0.1 copy.64
  154.2 1.0 fusion.23
  155.3 46.9 %custom-call.16 = f32[1,4,128,128]{3,2,1,0:T(8,128)S(1)} custom-call(f32[1,4,128,128]{3,2,1,0:T(8,128)S(1)} %fusion.23), custom_call_target="Cholesky" | custom-call | tf_op jit(solution)/shard_map/jit(cholesky)/cholesky | solution.py:12
  202.2 0.1 compare_reduce_fusion.1
  202.3 0.1 select_bitcast_fusion
  202.4 39.3 %custom-call.17 = f32[1,4,1,128,128]{3,4,2,1,0:T(8,128)S(1)} custom-call(f32[1,4,1,128,128]{4,3,2,1,0:T(8,128)S(1)} %select_bitcast_fusion), custom_call_target="InvertDiagBlocksLowerTriangular" | custom-call | tf_op jit(solution)/shard_map/triangular_solve | solution.py:14
  241.8 0.6 fusion.21
  242.3 1.3 fusion.45
  243.7 0.0 all-gather.3.cloned.1.call-update
  243.7 0.3 all-reduce.5.cloned.1.call-start
  243.9 27.9 %all-gather.3.cloned.1.call-done = f32[16,128,128]{2,1,0:T(8,128)} async-done(((f32[4,128,128]{2,1,0:T(8,128)}), f32[16,128,128]{2,1,0:T(8,128)}) %all-gather.3.cloned.1.call-update) | async-done | bytes 1048592 | tf_op jit(solution)/shard_map/all_gather | solution.py:52
  271.8 3.3 %convolution_bitcast_fusion = f32[8,8,128,128]{3,1,0,2:T(8,128)S(1)} fusion(f32[16,128,128,1]{2,1,0,3:T(8,128)} %bitcast.85, s32[8,8]{1,0:T(8,128)S(1)} %bitcast.87), kind=kOutput, calls=%fused_computation.4 | convolution fusion | flops 201327616 | bytes 5243136 | tf_op jit(solution)/shard_map/shjx,hxcd->shjcd/dot_general | solution.py:55
  275.1 6.0 %fusion = f32[8,8,48,128]{3,2,1,0:T(8,128)S(1)} fusion(f32[8,8,128,48]{2,3,1,0:T(8,128)S(1)} %fusion.10, f32[8,8,128,128]{3,1,0,2:T(8,128)S(1)} %convolution_bitcast_fusion), kind=kOutput, calls=%fused_computation | convolution fusion | flops 603979776 | bytes 7340032 | tf_op jit(solution)/shard_map/shjac,shjcd->shjad/dot_general | solution.py:56
  281.1 2.4 fusion.15
  283.5 0.0 all-reduce.5.cloned.1.call-update
  283.5 0.1 copy.70
  283.7 0.1 convert_element_type.47
  283.8 21.7 %all-reduce.5.cloned.1.call-done = f32[8,48,48]{1,2,0:T(8,128)} async-done(((f32[8,48,48]{1,2,0:T(8,128)}), f32[8,48,48]{1,2,0:T(8,128)}) %all-reduce.5.cloned.1.call-update) | async-done | bytes 73744 | tf_op jit(solution)/shard_map/psum | solution.py:58
  305.5 1.4 fusion.26
  306.9 0.4 convolution_multiply_fusion
  307.4 0.1 copy.73
  307.5 0.8 reshape.185
  (17 shorter events, 0.2 us)
Async XLA Ops:
  7.2 112.8 %reduce-scatter.2.cloned.1.call-start = ((), (), s32[]{:S(2)}) async-start(), calls=%async_computation.1 | async-start | bytes 1310720 | tf_op jit(solution)/shard_map/reduce_scatter | solution.py:49
  9.2 66.4 %copy-start = (f32[8,1,8,48,128]{4,3,2,1,0:T(8,128)S(1)}, f32[8,1,8,48,128]{4,3,2,1,0:T(8,128)}, u32[]{:S(2)}) copy-start(f32[8,1,8,48,128]{4,3,2,1,0:T(8,128)} %param.7) | copy-start | bytes 4718596
  77.3 6.9 %copy-start.2 = (s32[8,1,8]{2,1,0:T(1,128)S(1)}, s32[8,1,8]{2,1,0:T(1,128)}, u32[]{:S(2)}) copy-start(s32[8,1,8]{2,1,0:T(1,128)} %param.9) | copy-start | bytes 772
  88.3 64.8 %copy-start.3 = (f32[1,4,128]{2,1,0:T(4,128)S(1)}, f32[1,4,128]{2,1,0:T(4,128)}, u32[]{:S(2)}) copy-start(f32[1,4,128]{2,1,0:T(4,128)} %param.10) | copy-start | bytes 6148
  89.8 63.3 %all-reduce.3.cloned.1.call-start = ((), (), s32[]{:S(2)}) async-start(), calls=%async_computation.2 | async-start | bytes 524288 | tf_op jit(solution)/shard_map/psum | solution.py:50
  120.0 151.8 %all-gather.3.cloned.1.call-start = ((), (), s32[]{:S(2)}) async-start(), calls=%async_computation.4 | async-start | bytes 1310720 | tf_op jit(solution)/shard_map/all_gather | solution.py:52
  243.7 61.8 %all-reduce.5.cloned.1.call-start = ((), (), s32[]{:S(2)}) async-start(), calls=%async_computation.3 | async-start | bytes 393216 | tf_op jit(solution)/shard_map/psum | solution.py:58
  281.1 2.5 copy-start.1
Sparse Core Ops, SparseCore 0:
  89.9 29.9 reduce-scatter.1
  122.3 30.7 all-reduce.2
  243.8 27.9 all-gather.2
  283.6 21.7 all-reduce.4
where the time goes:
time: 315 us
  other arithmetic  154 us (49%)
  waiting for transfers between devices  113 us (36%)
  matrix products  29.1 us (9%)
  between operations  14.1 us (4%)
  local copies, waits for them, and re-layouts  4.08 us (1%)
    another operation x8, other arithmetic, spd_inverse(): factor = jnp.linalg.cholesky(matrix)  82.4 us
    another operation x6, other arithmetic, spd_inverse(): lax.linalg.triangular_solve(factor, identity, left_side=True, lower=True)  69.1 us
    psum x1, waiting for transfers between devices, local(): block_sum = lax.psum(local_sum, 'group')  32.9 us
    reduce_scatter x1, waiting for transfers between devices, local(): lax.psum_scatter(block_table, 'station', scatter_dimension=1, tiled=True)  30.1 us
    all_gather x1, waiting for transfers between devices, local(): segment = lax.all_gather(bias_cov, 'station', axis=1, tiled=True)  27.9 us
    psum x1, waiting for transfers between devices, local(): combined = lax.psum(bias_part.reshape(bias_part.shape[0], -1), 'bias')  21.7 us
    dot_general x1, matrix products, local(): jnp.einsum('shjac,shjad->shjcd', weighted, weighted - solved, precision=p...  6.89 us
  transfers between devices with their start and end apart: 4, of which 4 were waited for; matrix products, arithmetic and copies ran while one was open for 0% of the time, Pallas kernels for 0%

commit v1 on v0

--- a/solution.py
+++ b/solution.py
@@ -55,7 +55,8 @@
     chosen = jnp.einsum("shjx,hxcd->shjcd", local_pick, segment, precision=precise)
     lifted = jnp.einsum("shjac,shjcd->shjad", solved, chosen, precision=precise)
     bias_part = jnp.einsum("shjad,shjbd->sab", lifted, solved, precision=precise)
-    combined = lax.psum(bias_part.reshape(bias_part.shape[0], -1), "bias")
+    load = bias_part.reshape(bias_part.shape[0], -1)
+    combined = lax.all_gather(load, axis_name="bias").sum(axis=0)
     amb_cov = finish_cov(keep_mask, inverse, combined.reshape(bias_part.shape), unimod)
     return (bias_cov, amb_cov)
 

time: 315 us -> 297 us (0.943)
  waiting for transfers between devices: 113 us -> 91 us
  blocking collectives: 0 us -> 5.02 us
    psum x1 -> x0, waiting for transfers between devices: 21.7 us -> none  [local(): combined = lax.psum(bias_part.reshape(bias_part.shape[0], -1), 'bias')]
    all_gather x0 -> x1, blocking collectives: none -> 5.02 us  [local(): combined = lax.all_gather(load, axis_name='bias').sum(axis=0)]
  transfers between devices with their start and end apart: 4 -> 3, of which waited for: 4 -> 3; matrix products, arithmetic and copies ran while one was open for 0% -> 0% of each run, Pallas kernels for 0% -> 0%
where the time goes in v1:
time: 297 us
  other arithmetic  155 us (52%)
  waiting for transfers between devices  91 us (31%)
  matrix products  27.4 us (9%)
  between operations  14.1 us (5%)
  blocking collectives  5.02 us (2%)
  local copies, waits for them, and re-layouts  4.41 us (1%)
    another operation x8, other arithmetic, spd_inverse(): factor = jnp.linalg.cholesky(matrix)  82.4 us
    another operation x6, other arithmetic, spd_inverse(): lax.linalg.triangular_solve(factor, identity, left_side=True, lower=True)  69.3 us
    psum x1, waiting for transfers between devices, local(): block_sum = lax.psum(local_sum, 'group')  32.9 us
    reduce_scatter x1, waiting for transfers between devices, local(): lax.psum_scatter(block_table, 'station', scatter_dimension=1, tiled=True)  30.1 us
    all_gather x1, waiting for transfers between devices, local(): segment = lax.all_gather(bias_cov, 'station', axis=1, tiled=True)  27.9 us
    dot_general x1, matrix products, local(): jnp.einsum('shjac,shjad->shjcd', weighted, weighted - solved, precision=p...  6.9 us
    dot_general x1, matrix products, local(): lifted = jnp.einsum('shjac,shjcd->shjad', solved, chosen, precision=precise)  5.96 us
  transfers between devices with their start and end apart: 3, of which 3 were waited for; matrix products, arithmetic and copies ran while one was open for 0% of the time, Pallas kernels for 0%

profile of v1, /device:TPU:0, one launch (start us, length us, event | category | flops | bytes accessed | tf_op | source)
XLA Modules:
  0.0 296.6 jit_solution(14959452669123224042)
XLA Ops:
  7.2 0.0 reduce-scatter.2.cloned.1.call-start
  7.3 0.7 fusion.43
  8.0 0.1 copy.57
  8.1 1.0 reshape.174
  9.1 0.1 copy.56
  9.2 0.1 fusion.24
  9.3 0.1 copy.58
  9.4 0.1 fusion.30
  9.6 35.2 %custom-call.14 = f32[8,48,48]{2,1,0:T(8,128)S(1)} custom-call(f32[8,48,48]{2,1,0:T(8,128)S(1)} %fusion.30), custom_call_target="Cholesky" | custom-call | tf_op jit(solution)/shard_map/jit(cholesky)/cholesky | solution.py:12
  44.8 0.1 compare_reduce_fusion
  44.9 0.1 select_bitcast_fusion.1
  45.0 29.5 %custom-call.15 = f32[8,1,48,48]{2,3,1,0:T(8,128)S(1)} custom-call(f32[8,1,48,48]{3,2,1,0:T(8,128)S(1)} %select_bitcast_fusion.1), custom_call_target="InvertDiagBlocksLowerTriangular" | custom-call | tf_op jit(solution)/shard_map/triangular_solve | solution.py:14
  74.6 0.5 fusion.28
  75.1 0.5 fusion.44
  75.6 1.7 fusion.10
  77.2 6.9 %fusion.7 = f32[8,8,128,128]{3,2,1,0:T(8,128)S(1)} fusion(f32[8,8,128,48]{2,3,1,0:T(8,128)S(1)} %fusion.10, f32[8,1,8,48,128]{4,3,2,1,0:T(8,128)S(1)} %copy-done, f32[8,48]{1,0:T(8,128)S(1)} %fusion.43), kind=kOutput, calls=%fused_computation.9 | convolution fusion | flops 605159424 | bytes 7341568 | tf_op jit(solution)/shard_map/shjac,shjad->shjcd/dot_general | solution.py:43
  84.2 4.1 %fusion.12 = f32[16,128,128]{2,0,1:T(8,128)S(1)} fusion(f32[8,8,128,128]{3,2,1,0:T(8,128)S(1)} %fusion.7, s32[8,8]{1,0:T(8,128)S(1)} %bitcast.87), kind=kOutput, calls=%fused_computation.14 | convolution fusion | flops 201327616 | bytes 5243136 | tf_op jit(solution)/shard_map/shjx,shjcd->hxcd/dot_general | solution.py:48
  88.3 1.4 copy.63
  89.7 0.0 reduce-scatter.2.cloned.1.call-update
  89.7 0.0 all-reduce.2.cloned.1.call-start
  89.8 30.1 %reduce-scatter.2.cloned.1.call-done = f32[1,4,128,128]{2,3,1,0:T(8,128)} async-done(((f32[1,16,128,128]{2,3,1,0:T(8,128)}), f32[1,4,128,128]{2,3,1,0:T(8,128)}) %reduce-scatter.2.cloned.1.call-update) | async-done | bytes 262160 | tf_op jit(solution)/shard_map/reduce_scatter | solution.py:49
  119.9 0.0 all-reduce.2.cloned.1.call-update
  119.9 0.0 all-gather.3.cloned.1.call-start
  120.0 0.1 copy.64
  120.1 32.9 %all-reduce.2.cloned.1.call-done = f32[1,4,128,128]{2,3,1,0:T(8,128)} async-done(((f32[1,4,128,128]{2,3,1,0:T(8,128)}), f32[1,4,128,128]{2,3,1,0:T(8,128)}) %all-reduce.2.cloned.1.call-update) | async-done | bytes 262160 | tf_op jit(solution)/shard_map/psum | solution.py:50
  153.1 1.0 multiply_add_fusion
  154.0 0.1 copy.65
  154.2 1.0 fusion.23
  155.2 46.9 %custom-call.16 = f32[1,4,128,128]{3,2,1,0:T(8,128)S(1)} custom-call(f32[1,4,128,128]{3,2,1,0:T(8,128)S(1)} %fusion.23), custom_call_target="Cholesky" | custom-call | tf_op jit(solution)/shard_map/jit(cholesky)/cholesky | solution.py:12
  202.1 0.1 compare_reduce_fusion.1
  202.2 0.1 select_bitcast_fusion
  202.3 39.5 %custom-call.17 = f32[1,4,1,128,128]{3,4,2,1,0:T(8,128)S(1)} custom-call(f32[1,4,1,128,128]{4,3,2,1,0:T(8,128)S(1)} %select_bitcast_fusion), custom_call_target="InvertDiagBlocksLowerTriangular" | custom-call | tf_op jit(solution)/shard_map/triangular_solve | solution.py:14
  241.9 0.6 fusion.21
  242.5 1.3 fusion.45
  243.8 0.1 copy.70
  244.0 0.1 convert_element_type.47
  244.1 27.9 %all-gather.3.cloned.1.call-done = f32[16,128,128]{2,1,0:T(8,128)} async-done(((f32[4,128,128]{2,1,0:T(8,128)}), f32[16,128,128]{2,1,0:T(8,128)}) %all-gather.3.cloned.1.call-update) | async-done | bytes 1048592 | tf_op jit(solution)/shard_map/all_gather | solution.py:52
  272.0 3.3 %convolution_bitcast_fusion = f32[8,8,128,128]{3,1,0,2:T(8,128)S(1)} fusion(f32[16,128,128,1]{2,1,0,3:T(8,128)} %bitcast.86, s32[8,8]{1,0:T(8,128)S(1)} %bitcast.88), kind=kOutput, calls=%fused_computation.4 | convolution fusion | flops 201327616 | bytes 5243136 | tf_op jit(solution)/shard_map/shjx,hxcd->shjcd/dot_general | solution.py:55
  275.3 6.0 %fusion = f32[8,8,48,128]{3,2,1,0:T(8,128)S(1)} fusion(f32[8,8,128,48]{2,3,1,0:T(8,128)S(1)} %fusion.10, f32[8,8,128,128]{3,1,0,2:T(8,128)S(1)} %convolution_bitcast_fusion), kind=kOutput, calls=%fused_computation | convolution fusion | flops 603979776 | bytes 7340032 | tf_op jit(solution)/shard_map/shjac,shjcd->shjad/dot_general | solution.py:56
  281.2 1.6 fusion.15
  282.8 0.1 all_gather_reshape.3
  283.0 5.0 %all_gather.7 = f32[2,8,2304]{2,1,0:T(8,128)S(1)} all-gather(f32[1,8,2304]{2,1,0:T(8,128)S(1)} %all_gather_reshape.3), channel_id=1, replica_groups=mesh['station'=4,'group'=4,'bias'=2] {'bias'}, dimensions={0}, use_global_device_ids=true | all-gather | bytes 221184 | tf_op jit(solution)/shard_map/all_gather | solution.py:59
  288.0 0.1 reshape.180
  288.1 0.1 copy.71
  288.2 0.5 fusion.26
  288.8 0.4 convolution_multiply_fusion
  289.2 0.1 copy.74
  289.3 0.8 reshape.181
  (19 shorter events, 0.2 us)
Async XLA Ops:
  7.2 112.7 %reduce-scatter.2.cloned.1.call-start = ((), (), s32[]{:S(2)}) async-start(), calls=%async_computation.1 | async-start | bytes 1310720 | tf_op jit(solution)/shard_map/reduce_scatter | solution.py:49
  9.2 66.4 %copy-start = (f32[8,1,8,48,128]{4,3,2,1,0:T(8,128)S(1)}, f32[8,1,8,48,128]{4,3,2,1,0:T(8,128)}, u32[]{:S(2)}) copy-start(f32[8,1,8,48,128]{4,3,2,1,0:T(8,128)} %param.7) | copy-start | bytes 4718596
  77.2 6.9 %copy-start.2 = (s32[8,1,8]{2,1,0:T(1,128)S(1)}, s32[8,1,8]{2,1,0:T(1,128)}, u32[]{:S(2)}) copy-start(s32[8,1,8]{2,1,0:T(1,128)} %param.9) | copy-start | bytes 772
  88.3 64.8 %copy-start.3 = (f32[1,4,128]{2,1,0:T(4,128)S(1)}, f32[1,4,128]{2,1,0:T(4,128)}, u32[]{:S(2)}) copy-start(f32[1,4,128]{2,1,0:T(4,128)} %param.10) | copy-start | bytes 6148
  89.7 63.3 %all-reduce.2.cloned.1.call-start = ((), (), s32[]{:S(2)}) async-start(), calls=%async_computation.2 | async-start | bytes 524288 | tf_op jit(solution)/shard_map/psum | solution.py:50
  119.9 152.0 %all-gather.3.cloned.1.call-start = ((), (), s32[]{:S(2)}) async-start(), calls=%async_computation.3 | async-start | bytes 1310720 | tf_op jit(solution)/shard_map/all_gather | solution.py:52
  155.2 88.8 %copy-start.1 = (s32[8,2304]{1,0:T(8,128)S(1)}, s32[8,2304]{1,0:T(8,128)}, u32[]{:S(2)}) copy-start(s32[8,2304]{1,0:T(8,128)} %param.11) | copy-start | bytes 221188
Sparse Core Ops, SparseCore 0:
  89.9 29.9 reduce-scatter.1
  122.2 30.7 all-reduce.1
  243.9 27.9 all-gather.2
